TPU v7x, 32 devices: a whole 2x2x4 slice. The times are simulated.
32 devices in a mesh: ctx: 4 (over z), tp: 2 (over x), dp: 4 (over y, core).
Axes of the slice: x: 2, y: 2, z: 4, core: 2. Of those that a mesh axis runs over, the one named last changes fastest.
Arguments:
- queries: bfloat16 [4, 1024, 8192], P('dp', 'ctx', 'tp'), may hold values from -80 to 80
- prompt_keys: bfloat16 [4, 1024, 1024], P('dp', 'ctx', 'tp'), may hold values from -4 to 4
- prompt_values: bfloat16 [4, 1024, 1024], P('dp', 'ctx', 'tp'), may hold values from -6 to 6
- resp_keys: bfloat16 [4, 1024, 1024], P('dp', 'ctx', 'tp'), may hold values from -4 to 4
- resp_values: bfloat16 [4, 1024, 1024], P('dp', 'ctx', 'tp'), may hold values from -6 to 6
- pattern: int32 [4, 2, 8], P('dp'), may hold values from 0 to 1, as said below
- lengths: int32 [4, 2], P('dp'), may hold values from 257 to 512, as said below
- out_weight: bfloat16 [8192, 4096], P(('tp', 'dp'), 'ctx'), may hold values from -0.0625 to 0.0625
Outputs:
- attended: bfloat16 [4, 1024, 4096], P('dp', 'ctx', 'tp')
Inputs may be any that keep to these rules, and one draw needn't show every extreme that they name: pattern[g, r, 0] is 1 for every response; each response reads 4 or more blocks; in each group some response reads all 8 blocks. `lengths`: in each group some response has length 512.
All inputs are finite; a program needn't handle non-finite values.
Results may differ from a plain program's by a relative error of at most 0.013.
Values may be sent and summed in bfloat16 or wider, within the bound.
A program may use at most 192 MiB of HBM per device.

v0:
```python
import jax
import jax.numpy as jnp
from jax import lax
from jax.sharding import PartitionSpec as P

HD = 128
BLK = 128
RLEN = 512


def shifted(x, axis, by):
    devices = lax.axis_size(axis)
    pairs = [(i, i + by) for i in range(devices) if 0 <= i + by < devices]
    return lax.ppermute(x, axis, pairs)


def local(
    queries, prompt_keys, prompt_values, resp_keys, resp_values, pattern, lengths, out_weight
):
    tok = queries.shape[1]
    kv_here = prompt_keys.shape[2] // HD
    q_here = queries.shape[2] // HD
    group = q_here // kv_here
    scale = HD ** (-0.5)
    halves = RLEN // tok
    responses = lax.axis_size("ctx") // halves
    place = lax.axis_index("ctx")
    resp_id = place % responses
    half = place // responses
    positions = half * tok + jnp.arange(tok, dtype=jnp.int32)
    chosen = jnp.arange(pattern.shape[1], dtype=jnp.int32) == resp_id
    block_row = jnp.sum(jnp.where(chosen[:, None], pattern[0], 0), axis=0)
    live_len = jnp.sum(jnp.where(chosen, lengths[0], 0))
    query_heads = queries[0].reshape(tok, kv_here, group, HD)
    earlier = shifted((resp_keys, resp_values), "ctx", responses)
    own_keys = jnp.concatenate([earlier[0][0], resp_keys[0]], axis=0).reshape(2 * tok, kv_here, HD)
    own_vals = jnp.concatenate([earlier[1][0], resp_values[0]], axis=0).reshape(
        2 * tok, kv_here, HD
    )
    key_pos = (half - 1) * tok + jnp.arange(2 * tok, dtype=jnp.int32)
    allowed = (key_pos[None, :] >= 0) & (key_pos[None, :] <= positions[:, None])
    scores = (
        jnp.einsum("ikgd,jkd->kgij", query_heads, own_keys, preferred_element_type=jnp.float32)
        * scale
    )
    running = jnp.max(jnp.where(allowed, scores, -jnp.inf), axis=-1)
    probs = jnp.where(allowed, jnp.exp(scores - running[..., None]), 0.0)
    total = jnp.sum(probs, axis=-1)
    accum = jnp.einsum(
        "kgij,jkd->kgid", probs.astype(jnp.bfloat16), own_vals, preferred_element_type=jnp.float32
    )
    pieces = (
        lax.all_gather(prompt_keys, "ctx", axis=1, tiled=True),
        lax.all_gather(prompt_values, "ctx", axis=1, tiled=True),
    )
    count = pieces[0].shape[1]
    block_ids = jnp.arange(count, dtype=jnp.int32) // BLK
    onehot = block_ids[:, None] == jnp.arange(block_row.shape[0], dtype=jnp.int32)[None, :]
    readable = jnp.sum(jnp.where(onehot, block_row[None, :], 0), axis=1) > 0
    piece_keys = pieces[0][0].reshape(-1, kv_here, HD)
    piece_vals = pieces[1][0].reshape(-1, kv_here, HD)
    block_scores = (
        jnp.einsum("ikgd,jkd->kgij", query_heads, piece_keys, preferred_element_type=jnp.float32)
        * scale
    )
    mask = readable[None, None, None, :]
    new_max = jnp.maximum(running, jnp.max(jnp.where(mask, block_scores, -jnp.inf), axis=-1))
    weights = jnp.where(mask, jnp.exp(block_scores - new_max[..., None]), 0.0)
    factor = jnp.exp(running - new_max)
    new_total = total * factor + jnp.sum(weights, axis=-1)
    new_acc = accum * factor[..., None] + jnp.einsum(
        "kgij,jkd->kgid",
        weights.astype(jnp.bfloat16),
        piece_vals,
        preferred_element_type=jnp.float32,
    )
    context = new_acc / new_total[..., None]
    context = jnp.transpose(context, (2, 0, 1, 3)).reshape(tok, q_here * HD)
    context = jnp.where((positions < live_len)[:, None], context, 0.0).astype(jnp.bfloat16)
    head_rows = lax.all_gather(out_weight, "dp", axis=0, tiled=True)
    rows = lax.all_gather(context, "ctx", axis=0, tiled=True)
    columns = jnp.dot(rows, head_rows, preferred_element_type=jnp.float32).astype(jnp.bfloat16)
    partial_out = lax.all_to_all(columns, "ctx", split_axis=0, concat_axis=1, tiled=True)
    summed = lax.psum_scatter(partial_out, "tp", scatter_dimension=1, tiled=True)
    return summed[None]


def solution(mesh):
    placed = (
        P("dp", "ctx", "tp"),
        P("dp", "ctx", "tp"),
        P("dp", "ctx", "tp"),
        P("dp", "ctx", "tp"),
        P("dp", "ctx", "tp"),
        P("dp", None, None),
        P("dp", None),
        P(("tp", "dp"), "ctx"),
    )
    return jax.shard_map(
        local, mesh=mesh, in_specs=placed, out_specs=P("dp", "ctx", "tp"), check_vma=False
    )
```

profile of v0, /device:TPU:0, one launch (start us, length us, event | category | flops | bytes accessed | tf_op | source)
XLA Modules:
  0.0 398.9 jit_solution(16821264540768724130)
XLA Ops:
  6.5 1.8 copy.39
  8.4 0.7 all-gather.7.cloned.1.call-update
  9.2 0.7 all-gather.11.cloned.1.call-update
  9.9 1.1 copy.31
  11.0 6.0 %collective-permute-start = (bf16[1,256,512]{1,2,0:T(8,128)(2,1)S(1)}, bf16[1,256,512]{1,2,0:T(8,128)(2,1)S(1)}, u32[]{:S(2)}, u32[]{:S(2)}) collective-permute-start(bf16[1,256,512]{1,2,0:T(8,128)(2,1)S(1)} %copy.31), channel_id=1, source_target_pairs={{0,16},{8,24},{1,17},{9,25},{2,18},{10,26},{3,19},{11,27},{4,20},{... | collective-permute-start | bytes 786440 | tf_op jit(solution)/shard_map/ppermute | solution.py:14
  17.0 1.3 collective-permute-start.1
  18.3 0.6 broadcast_compare_fusion.1
  18.9 1.3 fusion.33
  20.2 0.8 fusion.32
  21.1 0.6 broadcast_compare_fusion.2
  21.7 1.1 copy.37
  22.7 2.1 copy.54
  24.8 0.2 copy.34
  25.0 0.9 compare_and_fusion
  25.9 1.8 collective-permute-done
  27.7 0.2 copy.33
  27.8 10.0 %collective-permute-done.1 = bf16[1,256,512]{2,1,0:T(8,128)(2,1)S(1)} collective-permute-done((bf16[1,256,512]{2,1,0:T(8,128)(2,1)}, bf16[1,256,512]{2,1,0:T(8,128)(2,1)S(1)}, u32[]{:S(2)}, u32[]{:S(2)}) %collective-permute-start.1) | collective-permute-done | bytes 262176 | tf_op jit(solution)/shard_map/ppermute | solution.py:14
  38.0 7.2 %fusion.5 = (f32[4,8,256]{2,1,0:T(8,128)S(1)}, f32[4,512,256,8]{2,1,3,0:T(8,128)}) fusion(pred[256,512]{0,1:T(8,128)(4,1)S(1)} %compare_and_fusion, bf16[256,4,8,128]{3,2,1,0:T(8,128)(2,1)S(1)} %bitcast.101, bf16[256,4,128]{2,0,1:T(8,128)(2,1)S(1)} %copy.34, bf16[256,4,128]{2,0,1:T(8,128)(2,1)S(1)} %copy.33), kind=kOutput, calls=%fused_computation.9 | convolution fusion | flops 1087365120 | bytes 19562496 | tf_op jit(solution)/shard_map/ikgd,jkd->kgij/dot_general | solution.py:43
  45.2 9.2 %fusion.11 = f32[4,8,256]{2,1,0:T(8,128)S(1)} fusion(f32[4,512,256,8]{2,1,3,0:T(8,128)} %get-tuple-element.8, f32[4,8,256]{2,1,0:T(8,128)S(1)} %get-tuple-element.7, pred[256,512]{0,1:T(8,128)(4,1)S(1)} %compare_and_fusion), kind=kLoop, calls=%fused_computation.14 | loop fusion | flops 16769024 | bytes 16973824 | tf_op jit(solution)/shard_map/reduce_sum | solution.py:48
  54.4 16.1 %fusion = (f32[4,8,256]{2,1,0:T(8,128)S(1)}, f32[4,1024,256,8]{2,1,3,0:T(8,128)}) fusion(pred[1024]{0:T(1024)(128)(4,1)S(1)} %broadcast_compare_fusion, bf16[1024,4,128,1]{0,2,3,1:T(8,128)(2,1)} %bitcast.107, bf16[256,4,8,128]{3,2,1,0:T(8,128)(2,1)S(1)} %bitcast.102), kind=kOutput, calls=%fused_computation.2 | convolution fusion | flops 2172641280 | bytes 36733952 | tf_op jit(solution)/shard_map/ikgd,jkd->kgij/dot_general | solution.py:63
  70.4 14.8 %all-gather.7.cloned.1.call-done = bf16[1,1024,512]{2,1,0:T(8,128)(2,1)} async-done(((bf16[1,256,512]{2,1,0:T(8,128)(2,1)}), bf16[1,1024,512]{2,1,0:T(8,128)(2,1)}) %all-gather.7.cloned.1.call-update) | async-done | bytes 1048592 | tf_op jit(solution)/shard_map/all_gather | solution.py:54
  85.2 1.5 copy.42
  86.7 15.7 %fusion.3 = f32[4,8,256]{2,1,0:T(8,128)S(1)} fusion(f32[4,1024,256,8]{2,1,3,0:T(8,128)} %get-tuple-element.10, f32[4,8,256]{2,1,0:T(8,128)S(1)} %max.18, pred[1024]{0:T(1024)(128)(4,1)S(1)} %broadcast_compare_fusion), kind=kLoop, calls=%fused_computation.5 | loop fusion | flops 33546240 | bytes 33620992 | tf_op jit(solution)/shard_map/reduce_sum | solution.py:70
  102.4 14.2 %fusion.8 = f32[4,8,256,128]{2,3,1,0:T(8,128)S(1)} fusion(bf16[1024,4,128,1]{0,2,3,1:T(8,128)(2,1)S(1)} %bitcast.108, f32[4,1024,256,8]{2,1,3,0:T(8,128)} %get-tuple-element.10, f32[4,8,256]{2,1,0:T(8,128)S(1)} %max.18, pred[1024]{0:T(1024)(128)(4,1)S(1)} %broadcast_compare_fusion), kind=kOutput, calls=%fused_computation.12 | convolution fusion | flops 2181038080 | bytes 38831104 | tf_op jit(solution)/shard_map/kgij,jkd->kgid/dot_general | solution.py:71
  116.6 7.9 %fusion.17 = bf16[256,4,8,128]{0,3,2,1:T(8,128)(2,1)S(1)} fusion(f32[4,8,256,128]{2,3,1,0:T(8,128)S(1)} %fusion.8, f32[4,512,256,8]{2,1,3,0:T(8,128)} %get-tuple-element.8, f32[4,8,256]{2,1,0:T(8,128)S(1)} %get-tuple-element.7, pred[256,512]{0,1:T(8,128)(4,1)S(1)} %compare_and_fusion, f32[256,4,8]{0,2,1:T(8,128)S(1)} %get-tuple-element.5, ...), kind=kOutput, calls=%fused_computation.21 | convolution fusion | flops 1095761920 | bytes 23822336 | tf_op jit(solution)/shard_map/kgij,jkd->kgid/dot_general | solution.py:49
  124.6 1.9 fusion.16
  126.6 17.9 %all-gather.11.cloned.1.call-done = bf16[4096,1024]{1,0:T(8,128)(2,1)} async-done(((bf16[1024,1024]{1,0:T(8,128)(2,1)}), bf16[4096,1024]{1,0:T(8,128)(2,1)}) %all-gather.11.cloned.1.call-update) | async-done | bytes 8388624 | tf_op jit(solution)/shard_map/all_gather | solution.py:80
  144.5 150.6 %all-gather.9.cloned.1.call-done = bf16[1024,4096]{0,1:T(8,128)(2,1)} async-done(((bf16[256,4096]{0,1:T(8,128)(2,1)}), bf16[1024,4096]{0,1:T(8,128)(2,1)}) %all-gather.9.cloned.1.call-update) | async-done | bytes 8388624 | tf_op jit(solution)/shard_map/all_gather | solution.py:81
  295.0 13.7 %convolution_convert_fusion = bf16[1024,1024]{1,0:T(8,128)(2,1)S(1)} fusion(bf16[1024,4096]{0,1:T(8,128)(2,1)} %all-gather.9.cloned.1.call-done, bf16[4096,1024]{1,0:T(8,128)(2,1)} %all-gather.11.cloned.1.call-done), kind=kOutput, calls=%fused_computation.23 | convolution fusion | flops 8590983168 | bytes 18874368 | tf_op jit(solution)/shard_map/dot_general | solution.py:82
  308.8 50.8 %all_to_all.19 = bf16[4,256,1024]{2,1,0:T(8,128)(2,1)S(1)} all-to-all(bf16[4,256,1024]{2,1,0:T(8,128)(2,1)S(1)} %bitcast.106), channel_id=1, replica_groups=mesh['ctx'=4,'tp'=2,'dp'=4] {'ctx'}, dimensions={0} | all-to-all | bytes 4194304 | tf_op jit(solution)/shard_map/all_to_all | solution.py:83
  359.5 1.5 copy.53
  361.1 31.3 %reduce-scatter.2.cloned.1.call-done = bf16[256,2048]{1,0:T(8,128)(2,1)} async-done(((bf16[256,4096]{1,0:T(8,128)(2,1)}), bf16[256,2048]{1,0:T(8,128)(2,1)}) %reduce-scatter.2.cloned.1.call-update) | async-done | bytes 1048592 | tf_op jit(solution)/shard_map/reduce_scatter | solution.py:84
  (18 shorter events, 0.5 us)
Async XLA Ops:
  6.5 47.8 %all-gather.5.cloned.1.call-start = ((), (), s32[]{:S(2)}) async-start(), calls=%async_computation.2 | async-start | bytes 1310720 | tf_op jit(solution)/shard_map/all_gather | solution.py:53
  8.4 76.9 %all-gather.7.cloned.1.call-start = ((), (), s32[]{:S(2)}) async-start(), calls=%async_computation.3 | async-start | bytes 1310720 | tf_op jit(solution)/shard_map/all_gather | solution.py:54
  9.1 135.4 %all-gather.11.cloned.1.call-start = ((), (), s32[]{:S(2)}) async-start(), calls=%async_computation.5 | async-start | bytes 10485760 | tf_op jit(solution)/shard_map/all_gather | solution.py:80
  9.8 285.2 %all-gather.9.cloned.1.call-start = ((), (), s32[]{:S(2)}) async-start(), calls=%async_computation.4 | async-start | bytes 10485760 | tf_op jit(solution)/shard_map/all_gather | solution.py:81
  11.0 16.7 %collective-permute-start = (bf16[1,256,512]{1,2,0:T(8,128)(2,1)S(1)}, bf16[1,256,512]{1,2,0:T(8,128)(2,1)S(1)}, u32[]{:S(2)}, u32[]{:S(2)}) collective-permute-start(bf16[1,256,512]{1,2,0:T(8,128)(2,1)S(1)} %copy.31), channel_id=1, source_target_pairs={{0,16},{8,24},{1,17},{9,25},{2,18},{10,26},{3,19},{11,27},{4,20},{... | collective-permute-start | bytes 786440 | tf_op jit(solution)/shard_map/ppermute | solution.py:14
  17.0 20.9 %collective-permute-start.1 = (bf16[1,256,512]{2,1,0:T(8,128)(2,1)}, bf16[1,256,512]{2,1,0:T(8,128)(2,1)S(1)}, u32[]{:S(2)}, u32[]{:S(2)}) collective-permute-start(bf16[1,256,512]{2,1,0:T(8,128)(2,1)} %param.12), channel_id=1, source_target_pairs={{0,16},{8,24},{1,17},{9,25},{2,18},{10,26},{3,19},{11,27},{4,20},{... | collective-permute-start | bytes 786440 | tf_op jit(solution)/shard_map/ppermute | solution.py:14
  126.5 265.9 %reduce-scatter.2.cloned.1.call-start = ((), (), s32[]{:S(2)}) async-start(), calls=%async_computation.6 | async-start | bytes 3145728 | tf_op jit(solution)/shard_map/reduce_scatter | solution.py:84
Sparse Core Ops, SparseCore 0:
  8.9 44.7 all-gather.4
  55.2 29.9 all-gather.6
  86.8 57.6 all-gather.10
  145.9 149.0 all-gather.8
  361.2 31.1 reduce-scatter.1
where the time goes:
time: 399 us
  waiting for transfers between devices  228 us (57%)
  matrix products  59.1 us (15%)
  blocking collectives  50.8 us (13%)
  other arithmetic  31 us (8%)
  between operations  13.3 us (3%)
  local copies, waits for them, and re-layouts  9.5 us (2%)
  starting transfers between devices  7.45 us (2%)
    all_gather x1, waiting for transfers between devices, local(): rows = lax.all_gather(context, 'ctx', axis=0, tiled=True)  151 us
    all_to_all x1, blocking collectives, local(): lax.all_to_all(columns, 'ctx', split_axis=0, concat_axis=1, tiled=True)  50.8 us
    reduce_scatter x1, waiting for transfers between devices, local(): lax.psum_scatter(partial_out, 'tp', scatter_dimension=1, tiled=True)  31.3 us
    all_gather x1, waiting for transfers between devices, local(): head_rows = lax.all_gather(out_weight, 'dp', axis=0, tiled=True)  17.9 us
    dot_general x1, matrix products, local(): jnp.einsum('ikgd,jkd->kgij', query_heads, piece_keys, preferred_element_t...  16.1 us
    reduce_sum x1, other arithmetic, local(): new_total = total * factor + jnp.sum(weights, axis=-1)  15.7 us
    all_gather x1, waiting for transfers between devices, local(): lax.all_gather(prompt_values, 'ctx', axis=1, tiled=True)  14.8 us
    dot_general x1, matrix products, local(): jnp.einsum('kgij,jkd->kgid', weights.astype(jnp.bfloat16), piece_vals, pr...  14.2 us
  transfers between devices with their start and end apart: 7, of which 6 were waited for; matrix products, arithmetic and copies ran while one was open for 21% of the time, Pallas kernels for 0%

commit v1 on v0

--- a/solution.py
+++ b/solution.py
@@ -6,6 +6,19 @@
 HD = 128
 BLK = 128
 RLEN = 512
+
+
+def gather_around(value, axis, dim):
+    ways = lax.axis_size(axis)
+    up = [(d, (d + 1) % ways) for d in range(ways)]
+    down = [(d, (d - 1) % ways) for d in range(ways)]
+    earlier, later = ([value], [value])
+    for _ in range(ways // 2):
+        earlier.append(lax.ppermute(earlier[-1], axis, up))
+    for _ in range((ways - 1) // 2):
+        later.append(lax.ppermute(later[-1], axis, down))
+    line = jnp.concatenate([*earlier[::-1], *later[1:]], axis=dim)
+    return jnp.roll(line, (lax.axis_index(axis) - ways // 2) * value.shape[dim], axis=dim)
 
 
 def shifted(x, axis, by):
@@ -51,7 +64,7 @@
     )
     pieces = (
         lax.all_gather(prompt_keys, "ctx", axis=1, tiled=True),
-        lax.all_gather(prompt_values, "ctx", axis=1, tiled=True),
+        gather_around(prompt_values, "ctx", 1),
     )
     count = pieces[0].shape[1]
     block_ids = jnp.arange(count, dtype=jnp.int32) // BLK

time: 399 us -> 395 us (0.990)
  waiting for transfers between devices: 228 us -> 204 us
  starting transfers between devices: 7.45 us -> 23.5 us
  local copies, waits for them, and re-layouts: 9.5 us -> 20.2 us
  matrix products: 59.1 us -> 52.8 us
    ppermute x0 -> x3, starting transfers between devices: none -> 18.5 us  [the longest x2 16.4 us: gather_around(): earlier.append(lax.ppermute(earlier[-1], axis, up))]
    all_gather x1, waiting for transfers between devices: 17.9 us -> 0.02 us  [local(): head_rows = lax.all_gather(out_weight, 'dp', axis=0, tiled=True)]
    all_gather x1 -> x0, waiting for transfers between devices: 14.8 us -> none  [local(): lax.all_gather(prompt_values, 'ctx', axis=1, tiled=True)]
    ppermute x2, waiting for transfers between devices: 11.8 us -> 21.5 us  [shifted(): return lax.ppermute(x, axis, pairs)]
    unnamed x4 -> x21, local copies, waits for them, and re-layouts: 6.02 us -> 15.2 us
    dot_general x1, matrix products: 7.16 us -> 2.77 us  [local(): jnp.einsum('ikgd,jkd->kgij', query_heads, own_keys, preferred_element_typ...]
  transfers between devices with their start and end apart: 7 -> 9, of which waited for: 6 -> 4; matrix products, arithmetic and copies ran while one was open for 21% -> 20% of each run, Pallas kernels for 0% -> 0%
where the time goes in v1:
time: 395 us
  waiting for transfers between devices  204 us (52%)
  matrix products  52.8 us (13%)
  blocking collectives  50.8 us (13%)
  other arithmetic  30.2 us (8%)
  starting transfers between devices  23.5 us (6%)
  local copies, waits for them, and re-layouts  20.2 us (5%)
  between operations  13.4 us (3%)
    all_gather x1, waiting for transfers between devices, local(): rows = lax.all_gather(context, 'ctx', axis=0, tiled=True)  150 us
    all_to_all x1, blocking collectives, local(): lax.all_to_all(columns, 'ctx', split_axis=0, concat_axis=1, tiled=True)  50.8 us
    reduce_scatter x1, waiting for transfers between devices, local(): lax.psum_scatter(partial_out, 'tp', scatter_dimension=1, tiled=True)  31.3 us
    ppermute x2, waiting for transfers between devices, shifted(): return lax.ppermute(x, axis, pairs)  21.5 us
    ppermute x2, starting transfers between devices, gather_around(): earlier.append(lax.ppermute(earlier[-1], axis, up))  16.4 us
    dot_general x1, matrix products, local(): jnp.einsum('ikgd,jkd->kgij', query_heads, piece_keys, preferred_element_t...  15.9 us
    dot_general x1, matrix products, local(): jnp.einsum('kgij,jkd->kgid', weights.astype(jnp.bfloat16), piece_vals, pr...  15.5 us
    unnamed x21, local copies, waits for them, and re-layouts  15.2 us
  transfers between devices with their start and end apart: 9, of which 4 were waited for; matrix products, arithmetic and copies ran while one was open for 20% of the time, Pallas kernels for 0%

profile of v1, /device:TPU:0, one launch (start us, length us, event | category | flops | bytes accessed | tf_op | source)
XLA Modules:
  0.0 394.6 jit_solution(4349211188845416957)
XLA Ops:
  6.5 1.8 copy.39
  8.4 0.7 all-gather.8.cloned.1.call-update
  9.1 3.1 collective-permute-start.2
  12.3 2.1 collective-permute-start.4
  14.3 1.1 copy.31
  15.4 3.6 collective-permute-start
  19.0 1.3 collective-permute-start.1
  20.9 1.3 fusion.33
  22.2 0.8 fusion.32
  23.1 0.7 broadcast_compare_fusion.2
  23.8 1.8 copy.37
  25.7 2.1 copy.54
  27.8 0.9 compare_and_fusion
  28.7 12.5 %collective-permute-done = bf16[1,256,512]{1,2,0:T(8,128)(2,1)} collective-permute-done((bf16[1,256,512]{1,2,0:T(8,128)(2,1)S(1)}, bf16[1,256,512]{1,2,0:T(8,128)(2,1)}, u32[]{:S(2)}, u32[]{:S(2)}) %collective-permute-start) | collective-permute-done | bytes 262176 | tf_op jit(solution)/shard_map/ppermute | solution.py:27
  41.2 1.1 copy.33
  42.3 9.1 %collective-permute-done.1 = bf16[1,256,512]{2,1,0:T(8,128)(2,1)S(1)} collective-permute-done((bf16[1,256,512]{2,1,0:T(8,128)(2,1)}, bf16[1,256,512]{2,1,0:T(8,128)(2,1)S(1)}, u32[]{:S(2)}, u32[]{:S(2)}) %collective-permute-start.1) | collective-permute-done | bytes 262176 | tf_op jit(solution)/shard_map/ppermute | solution.py:27
  51.4 0.8 copy.36
  52.2 13.3 %collective-permute-start.3 = (bf16[1,256,512]{2,1,0:T(8,128)(2,1)S(1)}, bf16[1,256,512]{2,1,0:T(8,128)(2,1)S(1)}, u32[]{:S(2)}, u32[]{:S(2)}) collective-permute-start(bf16[1,256,512]{2,1,0:T(8,128)(2,1)S(1)} %collective-permute-done.2), channel_id=1, source_target_pairs={{0,8},{8,16},{16,24},{24,0},{1,9},{9,17},{17,25},{25,1},{2,10},{10... | collective-permute-start | bytes 786440 | tf_op jit(solution)/shard_map/ppermute | solution.py:17
  65.5 2.8 fusion.5
  68.3 8.3 %copy-done = f32[4,512,256,8]{2,1,3,0:T(8,128)} copy-done((f32[4,512,256,8]{2,1,3,0:T(8,128)}, f32[4,512,256,8]{2,1,3,0:T(8,128)S(1)}, u32[]{:S(2)}) %copy-start) | copy-done | bytes 16777240
  76.6 5.0 %fusion.13 = f32[4,8,256,128]{2,3,1,0:T(8,128)} fusion(f32[4,512,256,8]{2,1,3,0:T(8,128)S(1)} %get-tuple-element.8, f32[4,8,256]{2,1,0:T(8,128)S(1)} %get-tuple-element.7, pred[256,512]{0,1:T(8,128)(4,1)S(1)} %compare_and_fusion, bf16[256,4,128]{0,2,1:T(8,128)(2,1)S(1)} %bitcast.110, bf16[256,4,128]{0,2,1:T(8,128)(2,1)S(1)} %bitcast.111), kind=kOutput, calls=%fused_computation.16 | convolution fusion | flops 1091567616 | bytes 21659648 | tf_op jit(solution)/shard_map/kgij,jkd->kgid/dot_general | solution.py:62
  81.6 9.3 %fusion.11 = f32[4,8,256]{2,1,0:T(8,128)S(1)} fusion(f32[4,512,256,8]{2,1,3,0:T(8,128)} %copy-done, f32[4,8,256]{2,1,0:T(8,128)S(1)} %get-tuple-element.7, pred[256,512]{0,1:T(8,128)(4,1)S(1)} %compare_and_fusion), kind=kLoop, calls=%fused_computation.14 | loop fusion | flops 16769024 | bytes 16973824 | tf_op jit(solution)/shard_map/reduce_sum | solution.py:61
  91.2 1.3 copy.42
  92.5 15.9 %fusion = (f32[4,8,256]{2,1,0:T(8,128)S(1)}, f32[4,1024,256,8]{2,1,3,0:T(8,128)}) fusion(pred[1024]{0:T(1024)(128)(4,1)S(1)} %broadcast_compare_fusion, bf16[1024,4,128,1]{0,2,3,1:T(8,128)(2,1)} %bitcast.107, bf16[256,4,8,128]{3,2,1,0:T(8,128)(2,1)S(1)} %bitcast.102), kind=kOutput, calls=%fused_computation.2 | convolution fusion | flops 2172641280 | bytes 36733952 | tf_op jit(solution)/shard_map/ikgd,jkd->kgij/dot_general | solution.py:76
  108.4 14.7 %fusion.3 = f32[4,8,256]{2,1,0:T(8,128)S(1)} fusion(f32[4,1024,256,8]{2,1,3,0:T(8,128)} %get-tuple-element.10, f32[4,8,256]{2,1,0:T(8,128)S(1)} %max.18, pred[1024]{0:T(1024)(128)(4,1)S(1)} %broadcast_compare_fusion), kind=kLoop, calls=%fused_computation.5 | loop fusion | flops 33546240 | bytes 33620992 | tf_op jit(solution)/shard_map/reduce_sum | solution.py:83
  123.1 15.5 %fusion.17 = bf16[256,4,8,128]{0,3,2,1:T(8,128)(2,1)S(1)} fusion(f32[4,8,256,128]{2,3,1,0:T(8,128)} %fusion.13, bf16[1024,4,128,1]{0,2,3,1:T(8,128)(2,1)S(1)} %bitcast.108, f32[4,1024,256,8]{2,1,3,0:T(8,128)} %get-tuple-element.10, f32[4,8,256]{2,1,0:T(8,128)S(1)} %max.18, pred[1024]{0:T(1024)(128)(4,1)S(1)} %broadcast_compare_fusion, ...), kind=kOutput, calls=%fused_computation.21 | convolution fusion | flops 2185232384 | bytes 40993792 | tf_op jit(solution)/shard_map/kgij,jkd->kgid/dot_general | solution.py:84
  138.6 1.9 fusion.16
  140.6 150.1 %all-gather.6.cloned.1.call-done = bf16[1024,4096]{0,1:T(8,128)(2,1)} async-done(((bf16[256,4096]{0,1:T(8,128)(2,1)}), bf16[1024,4096]{0,1:T(8,128)(2,1)}) %all-gather.6.cloned.1.call-update) | async-done | bytes 8388624 | tf_op jit(solution)/shard_map/all_gather | solution.py:94
  290.7 13.7 %convolution_convert_fusion = bf16[1024,1024]{1,0:T(8,128)(2,1)S(1)} fusion(bf16[1024,4096]{0,1:T(8,128)(2,1)} %all-gather.6.cloned.1.call-done, bf16[4096,1024]{1,0:T(8,128)(2,1)} %all-gather.8.cloned.1.call-done), kind=kOutput, calls=%fused_computation.23 | convolution fusion | flops 8590983168 | bytes 18874368 | tf_op jit(solution)/shard_map/dot_general | solution.py:95
  304.5 50.8 %all_to_all.19 = bf16[4,256,1024]{2,1,0:T(8,128)(2,1)S(1)} all-to-all(bf16[4,256,1024]{2,1,0:T(8,128)(2,1)S(1)} %bitcast.106), channel_id=1, replica_groups=mesh['ctx'=4,'tp'=2,'dp'=4] {'ctx'}, dimensions={0} | all-to-all | bytes 4194304 | tf_op jit(solution)/shard_map/all_to_all | solution.py:96
  355.3 1.5 copy.53
  356.8 31.3 %reduce-scatter.2.cloned.1.call-done = bf16[256,2048]{1,0:T(8,128)(2,1)} async-done(((bf16[256,4096]{1,0:T(8,128)(2,1)}), bf16[256,2048]{1,0:T(8,128)(2,1)}) %reduce-scatter.2.cloned.1.call-update) | async-done | bytes 1048592 | tf_op jit(solution)/shard_map/reduce_scatter | solution.py:97
  (40 shorter events, 1.3 us)
Async XLA Ops:
  6.5 86.0 %all-gather.4.cloned.1.call-start = ((), (), s32[]{:S(2)}) async-start(), calls=%async_computation.2 | async-start | bytes 1310720 | tf_op jit(solution)/shard_map/all_gather | solution.py:66
  8.3 132.3 %all-gather.8.cloned.1.call-start = ((), (), s32[]{:S(2)}) async-start(), calls=%async_computation.4 | async-start | bytes 10485760 | tf_op jit(solution)/shard_map/all_gather | solution.py:93
  9.1 281.6 %all-gather.6.cloned.1.call-start = ((), (), s32[]{:S(2)}) async-start(), calls=%async_computation.3 | async-start | bytes 10485760 | tf_op jit(solution)/shard_map/all_gather | solution.py:94
  9.1 43.1 %collective-permute-start.2 = (bf16[1,256,512]{2,1,0:T(8,128)(2,1)}, bf16[1,256,512]{2,1,0:T(8,128)(2,1)S(1)}, u32[]{:S(2)}, u32[]{:S(2)}) collective-permute-start(bf16[1,256,512]{2,1,0:T(8,128)(2,1)} %param.10), channel_id=1, source_target_pairs={{0,8},{8,16},{16,24},{24,0},{1,9},{9,17},{17,25},{25,1},{2,10},{10... | collective-permute-start | bytes 786440 | tf_op jit(solution)/shard_map/ppermute | solution.py:17
  12.3 78.7 %collective-permute-start.4 = (bf16[1,256,512]{2,1,0:T(8,128)(2,1)}, bf16[1,256,512]{2,1,0:T(8,128)(2,1)S(1)}, u32[]{:S(2)}, u32[]{:S(2)}) collective-permute-start(bf16[1,256,512]{2,1,0:T(8,128)(2,1)} %param.10), channel_id=1, source_target_pairs={{0,24},{8,0},{16,8},{24,16},{1,25},{9,1},{17,9},{25,17},{2,26},{10... | collective-permute-start | bytes 786440 | tf_op jit(solution)/shard_map/ppermute | solution.py:19
  15.4 25.7 %collective-permute-start = (bf16[1,256,512]{1,2,0:T(8,128)(2,1)S(1)}, bf16[1,256,512]{1,2,0:T(8,128)(2,1)}, u32[]{:S(2)}, u32[]{:S(2)}) collective-permute-start(bf16[1,256,512]{1,2,0:T(8,128)(2,1)S(1)} %copy.31), channel_id=1, source_target_pairs={{0,16},{8,24},{1,17},{9,25},{2,18},{10,26},{3,19},{11,27},{4,20},{... | collective-permute-start | bytes 786440 | tf_op jit(solution)/shard_map/ppermute | solution.py:27
  19.0 32.4 %collective-permute-start.1 = (bf16[1,256,512]{2,1,0:T(8,128)(2,1)}, bf16[1,256,512]{2,1,0:T(8,128)(2,1)S(1)}, u32[]{:S(2)}, u32[]{:S(2)}) collective-permute-start(bf16[1,256,512]{2,1,0:T(8,128)(2,1)} %param.12), channel_id=1, source_target_pairs={{0,16},{8,24},{1,17},{9,25},{2,18},{10,26},{3,19},{11,27},{4,20},{... | collective-permute-start | bytes 786440 | tf_op jit(solution)/shard_map/ppermute | solution.py:27
  52.2 38.6 %collective-permute-start.3 = (bf16[1,256,512]{2,1,0:T(8,128)(2,1)S(1)}, bf16[1,256,512]{2,1,0:T(8,128)(2,1)S(1)}, u32[]{:S(2)}, u32[]{:S(2)}) collective-permute-start(bf16[1,256,512]{2,1,0:T(8,128)(2,1)S(1)} %collective-permute-done.2), channel_id=1, source_target_pairs={{0,8},{8,16},{16,24},{24,0},{1,9},{9,17},{17,25},{25,1},{2,10},{10... | collective-permute-start | bytes 786440 | tf_op jit(solution)/shard_map/ppermute | solution.py:17
  65.5 11.1 %copy-start.3 = (bf16[1,256,512]{1,2,0:T(8,128)(2,1)S(1)}, bf16[1,256,512]{1,2,0:T(8,128)(2,1)}, u32[]{:S(2)}) copy-start(bf16[1,256,512]{1,2,0:T(8,128)(2,1)} %copy.37) | copy-start | bytes 786436
  65.5 11.1 %copy-start.4 = (bf16[1,256,512]{1,2,0:T(8,128)(2,1)S(1)}, bf16[1,256,512]{1,2,0:T(8,128)(2,1)}, u32[]{:S(2)}) copy-start(bf16[1,256,512]{1,2,0:T(8,128)(2,1)} %copy.36) | copy-start | bytes 786436
  68.3 8.3 %copy-start = (f32[4,512,256,8]{2,1,3,0:T(8,128)}, f32[4,512,256,8]{2,1,3,0:T(8,128)S(1)}, u32[]{:S(2)}) copy-start(f32[4,512,256,8]{2,1,3,0:T(8,128)S(1)} %get-tuple-element.8) | copy-start | bytes 50331652
  81.6 9.4 %copy-start.2 = (bf16[1,256,512]{2,1,0:T(8,128)(2,1)S(1)}, bf16[1,256,512]{2,1,0:T(8,128)(2,1)}, u32[]{:S(2)}) copy-start(bf16[1,256,512]{2,1,0:T(8,128)(2,1)} %param.10) | copy-start | bytes 786436
  108.4 14.7 %copy-start.1 = (bf16[1,1024,512]{1,2,0:T(8,128)(2,1)S(1)}, bf16[1,1024,512]{1,2,0:T(8,128)(2,1)}, u32[]{:S(2)}) copy-start(bf16[1,1024,512]{1,2,0:T(8,128)(2,1)} %copy.42) | copy-start | bytes 3145732
  140.6 247.6 %reduce-scatter.2.cloned.1.call-start = ((), (), s32[]{:S(2)}) async-start(), calls=%async_computation.5 | async-start | bytes 3145728 | tf_op jit(solution)/shard_map/reduce_scatter | solution.py:97
Sparse Core Ops, SparseCore 0:
  8.9 53.1 all-gather.3
  63.6 58.5 all-gather.7
  140.7 150.0 all-gather.5
  356.9 31.1 reduce-scatter.1
